TPU v7x, 32 devices: a whole 2x2x4 slice. The times are simulated.
32 devices in a mesh: row: 4 (over z), col: 4 (over x, core), chol: 2 (over y).
Axes of the slice: x: 2, y: 2, z: 4, core: 2. Of those that a mesh axis runs over, the one named last changes fastest.
Arguments:
- left_vectors: bfloat16 [64, 4608, 1536], P(None, ('col', 'chol'), 'row'), may hold values from -0.75 to 0.75
- right_vectors: bfloat16 [16, 4608, 1536], P(None, ('col', 'chol'), 'row'), may hold values from -0.0234375 to 0.0234375
- amplitudes: bfloat16 [8, 16, 64], replicated, may hold values from -6 to 6
Outputs:
- ladder: float32 [8, 1536, 1536], P('chol', 'row', 'col')
All inputs are finite; a program needn't handle non-finite values.
Results may differ from a plain program's by a relative error of at most 0.0029.
Values may be sent and summed in bfloat16 or wider, within the bound.
No kernel may reach another device: no remote copies, remote signals or barrier semaphores. Data moves between devices by JAX's collectives and lax.ppermute only.
A program may use at most 256 MiB of HBM per device.

v0:
```python
import jax
import jax.numpy as jnp
from jax import lax
from jax.sharding import PartitionSpec as P


def shards(left_vectors, right_vectors, amplitudes):
    pairs, d_block, c_block = amplitudes.shape
    amp_rows = amplitudes.reshape(pairs * d_block, c_block)
    width_a = left_vectors.shape[2]
    right_full = lax.all_gather(right_vectors, "row", axis=2, tiled=True)
    columns = lax.axis_size("col")
    width_b = right_full.shape[2] // columns
    vectors = left_vectors.shape[1]
    halved = jnp.dot(
        amp_rows,
        left_vectors.reshape(c_block, vectors * width_a),
        preferred_element_type=jnp.float32,
    ).astype(jnp.bfloat16)
    halved = halved.reshape(pairs, d_block * vectors, width_a)
    panel = right_full.reshape(d_block * vectors, columns, width_b)
    ladder = jnp.einsum("ika,kcb->ciab", halved, panel, preferred_element_type=jnp.float32)
    ladder = ladder.reshape(columns * pairs, width_a, width_b)
    return lax.psum_scatter(ladder, ("col", "chol"), scatter_dimension=0, tiled=True)


def solution(mesh):
    return jax.shard_map(
        shards,
        mesh=mesh,
        in_specs=(P(None, ("col", "chol"), "row"), P(None, ("col", "chol"), "row"), P()),
        out_specs=P("chol", "row", "col"),
        check_vma=False,
    )
```

profile of v0, /device:TPU:0, one launch (start us, length us, event | category | flops | bytes accessed | tf_op | source)
XLA Modules:
  0.0 779.7 jit_solution(12643023936817732366)
XLA Ops:
  6.5 0.0 copy-start
  6.5 0.0 all-gather.2.cloned.1.call-start
  6.5 0.7 all-gather.2.cloned.1.call-update
  7.3 0.0 reduce-scatter.2.cloned.1.call-start
  7.3 40.3 %copy.11 = bf16[8,8,576,384]{3,1,2,0:T(8,128)(2,1)} copy(bf16[8,8,576,384]{3,2,1,0:T(8,128)(2,1)} %bitcast.23) | data formatting | bytes 56623104
  47.6 0.0 copy-done
  47.6 38.6 %convolution_convert_fusion = bf16[128,221184]{1,0:T(8,128)(2,1)} fusion(bf16[128,64]{1,0:T(8,128)(2,1)S(1)} %bitcast.20, bf16[64,221184]{1,0:T(8,128)(2,1)} %bitcast.21), kind=kOutput, calls=%fused_computation | convolution fusion | flops 3652190208 | bytes 84951040 | tf_op jit(solution)/shard_map/dot_general | solution.py:15
  86.2 50.1 %reshape.17 = bf16[8,9216,384]{2,1,0:T(8,128)(2,1)} reshape(bf16[128,221184]{1,0:T(8,128)(2,1)} %convolution_convert_fusion) | data formatting | bytes 113246208 | tf_op jit(solution)/shard_map/reshape | solution.py:20
  136.3 351.5 %all-gather.2.cloned.1.call-done = bf16[16,576,1536]{2,1,0:T(8,128)(2,1)} async-done(((bf16[16,576,384]{2,1,0:T(8,128)(2,1)}), bf16[16,576,1536]{2,1,0:T(8,128)(2,1)}) %all-gather.2.cloned.1.call-update) | async-done | bytes 28311568 | tf_op jit(solution)/shard_map/all_gather | solution.py:11
  487.8 47.2 %reshape.18 = bf16[9216,4,384]{2,1,0:T(4,128)(2,1)} reshape(bf16[16,576,1536]{2,1,0:T(8,128)(2,1)} %all-gather.2.cloned.1.call-done) | data formatting | bytes 56623104 | tf_op jit(solution)/shard_map/reshape | solution.py:21
  535.0 0.0 copy-start.1
  535.0 100.5 %fusion.4 = f32[4,8,384,384]{3,2,0,1:T(8,128)} fusion(bf16[9216,4,384]{2,1,0:T(4,128)(2,1)} %reshape.18, bf16[8,9216,384]{2,1,0:T(8,128)(2,1)} %reshape.17), kind=kOutput, calls=%fused_computation.5 | convolution fusion | flops 86973087744 | bytes 103809024 | tf_op jit(solution)/shard_map/ika,kcb->ciab/dot_general | solution.py:22
  635.5 12.6 %copy.7 = f32[4,8,384,384]{3,2,1,0:T(8,128)} copy(f32[4,8,384,384]{3,2,0,1:T(8,128)} %fusion.4) | data formatting | bytes 37748736 | tf_op jit(solution)/shard_map/ika,kcb->ciab/transpose | solution.py:22
  648.1 0.0 reduce-scatter.2.cloned.1.call-update
  648.1 124.8 %reduce-scatter.2.cloned.1.call-done = f32[4,384,384]{2,1,0:T(8,128)} async-done(((f32[32,384,384]{2,1,0:T(8,128)}), f32[4,384,384]{2,1,0:T(8,128)}) %reduce-scatter.2.cloned.1.call-update) | async-done | bytes 2359312 | tf_op jit(solution)/shard_map/reduce_scatter | solution.py:24
  772.9 0.0 copy-done.1
Async XLA Ops:
  6.5 41.1 %copy-start = (bf16[8,16,64]{2,1,0:T(8,128)(2,1)S(1)}, bf16[8,16,64]{2,1,0:T(8,128)(2,1)}, u32[]{:S(2)}) copy-start(bf16[8,16,64]{2,1,0:T(8,128)(2,1)} %param.5) | copy-start | bytes 49156
  6.5 481.3 %all-gather.2.cloned.1.call-start = ((), (), s32[]{:S(2)}) async-start(), calls=%async_computation.1 | async-start | bytes 35389440 | tf_op jit(solution)/shard_map/all_gather | solution.py:11
  7.3 765.6 %reduce-scatter.2.cloned.1.call-start = ((), (), s32[]{:S(2)}) async-start(), calls=%async_computation.2 | async-start | bytes 21233664 | tf_op jit(solution)/shard_map/reduce_scatter | solution.py:24
  535.0 237.9 %copy-start.1 = (bf16[8,16,64]{2,1,0:T(8,128)(2,1)S(1)}, bf16[8,16,64]{2,1,0:T(8,128)(2,1)}, u32[]{:S(2)}) copy-start(bf16[8,16,64]{2,1,0:T(8,128)(2,1)} %param.5) | copy-start | bytes 49156
Sparse Core Ops, SparseCore 0:
  8.9 478.8 all-gather.1
  648.3 124.6 reduce-scatter.1
where the time goes:
time: 782 us; the launch traced here: 780 us
  waiting for transfers between devices  477 us (61%)
  local copies, waits for them, and re-layouts  150 us (19%)
  matrix products  139 us (18%)
  between operations  13.4 us (2%)
    all_gather x1, waiting for transfers between devices, shards(): right_full = lax.all_gather(right_vectors, 'row', axis=2, tiled=True)  352 us
    reduce_scatter x1, waiting for transfers between devices, shards(): lax.psum_scatter(ladder, ('col', 'chol'), scatter_dimension=0, tiled=True)  125 us
    dot_general x1, matrix products, shards(): jnp.einsum('ika,kcb->ciab', halved, panel, preferred_element_type=jnp.flo...  101 us
    reshape x1, local copies, waits for them, and re-layouts, shards(): halved = halved.reshape(pairs, d_block * vectors, width_a)  50.1 us
    reshape x1, local copies, waits for them, and re-layouts, shards(): panel = right_full.reshape(d_block * vectors, columns, width_b)  47.2 us
    unnamed x5, local copies, waits for them, and re-layouts  40.3 us
    dot_general x1, matrix products, shards(): jnp.dot(amp_rows, left_vectors.reshape(c_block, vectors * width_a), prefe...  38.6 us
  transfers between devices with their start and end apart: 2, of which 2 were waited for; matrix products, arithmetic and copies ran while one was open for 17% of the time, Pallas kernels for 0%

commit v1 on v0

--- a/solution.py
+++ b/solution.py
@@ -8,7 +8,9 @@
     pairs, d_block, c_block = amplitudes.shape
     amp_rows = amplitudes.reshape(pairs * d_block, c_block)
     width_a = left_vectors.shape[2]
-    right_full = lax.all_gather(right_vectors, "row", axis=2, tiled=True)
+    right_full = jnp.concatenate(
+        lax.all_to_all(jnp.stack([right_vectors] * lax.axis_size("row")), "row", 0, 0), axis=2
+    )
     columns = lax.axis_size("col")
     width_b = right_full.shape[2] // columns
     vectors = left_vectors.shape[1]

time: 782 us -> 887 us (1.13)
  waiting for transfers between devices: 477 us -> 609 us
  local copies, waits for them, and re-layouts: 150 us -> 117 us
  starting transfers between devices: 0.04 us -> 8.92 us
    all_to_all x0 -> x1, waiting for transfers between devices: none -> 483 us  [shards(): lax.all_to_all(jnp.stack([right_vectors] * lax.axis_size('row')), 'row',...]
    all_gather x1 -> x0, waiting for transfers between devices: 352 us -> none  [shards(): right_full = lax.all_gather(right_vectors, 'row', axis=2, tiled=True)]
    reshape x1 -> x0, local copies, waits for them, and re-layouts: 47.2 us -> none  [shards(): panel = right_full.reshape(d_block * vectors, columns, width_b)]
    another operation x0 -> x1, local copies, waits for them, and re-layouts: none -> 14.4 us  [shards(): jnp.stack([right_vectors] * lax.axis_size('row'))]
    all_to_all x0 -> x1, starting transfers between devices: none -> 8.87 us  [shards(): lax.all_to_all(jnp.stack([right_vectors] * lax.axis_size('row')), 'row',...]
  transfers between devices with their start and end apart: 2 -> 2, of which waited for: 2 -> 2; matrix products, arithmetic and copies ran while one was open for 17% -> 15% of each run, Pallas kernels for 0% -> 0%
where the time goes in v1:
time: 887 us; the launch traced here: 886 us
  waiting for transfers between devices  609 us (69%)
  matrix products  137 us (15%)
  local copies, waits for them, and re-layouts  117 us (13%)
  between operations  13.4 us (2%)
  starting transfers between devices  8.92 us (1%)
    all_to_all x1, waiting for transfers between devices, shards(): lax.all_to_all(jnp.stack([right_vectors] * lax.axis_size('row')), 'row',...  483 us
    reduce_scatter x1, waiting for transfers between devices, shards(): lax.psum_scatter(ladder, ('col', 'chol'), scatter_dimension=0, tiled=True)  126 us
    dot_general x1, matrix products, shards(): jnp.einsum('ika,kcb->ciab', halved, panel, preferred_element_type=jnp.flo...  98.8 us
    reshape x1, local copies, waits for them, and re-layouts, shards(): halved = halved.reshape(pairs, d_block * vectors, width_a)  50.1 us
    unnamed x5, local copies, waits for them, and re-layouts  40.3 us
    dot_general x1, matrix products, shards(): jnp.dot(amp_rows, left_vectors.reshape(c_block, vectors * width_a), prefe...  38.3 us
  transfers between devices with their start and end apart: 2, of which 2 were waited for; matrix products, arithmetic and copies ran while one was open for 15% of the time, Pallas kernels for 0%

profile of v1, /device:TPU:0, one launch (start us, length us, event | category | flops | bytes accessed | tf_op | source)
XLA Modules:
  0.0 885.6 jit_solution(5520400525623550320)
XLA Ops:
  6.5 0.0 copy-start
  6.5 14.4 %stack.2 = bf16[4,16,576,384]{3,2,1,0:T(8,128)(2,1)} broadcast(bf16[16,576,384]{2,1,0:T(8,128)(2,1)} %param.4), dimensions={1,2,3} | broadcast | bytes 35389440 | tf_op jit(solution)/shard_map/stack | solution.py:12
  21.0 8.9 %all-to-all-start = ((bf16[4,16,576,384]{3,2,1,0:T(8,128)(2,1)}), bf16[4,16,576,384]{3,2,1,0:T(8,128)(2,1)}, u32[]{:S(2)}, u32[]{:S(2)}) async-start(bf16[4,16,576,384]{3,2,1,0:T(8,128)(2,1)} %stack.2), calls=%async_computation | async-start | bytes 56623104 | tf_op jit(solution)/shard_map/all_to_all | solution.py:12
  29.9 0.0 reduce-scatter.2.cloned.1.call-start
  29.9 40.3 %copy.10 = bf16[8,8,576,384]{3,1,2,0:T(8,128)(2,1)} copy(bf16[8,8,576,384]{3,2,1,0:T(8,128)(2,1)} %bitcast.24) | data formatting | bytes 56623104
  70.2 0.0 copy-done
  70.2 38.3 %convolution_convert_fusion = bf16[128,221184]{1,0:T(8,128)(2,1)} fusion(bf16[128,64]{1,0:T(8,128)(2,1)S(1)} %bitcast.21, bf16[64,221184]{1,0:T(8,128)(2,1)} %bitcast.22), kind=kOutput, calls=%fused_computation | convolution fusion | flops 3652190208 | bytes 84951040 | tf_op jit(solution)/shard_map/dot_general | solution.py:17
  108.5 50.1 %reshape.19 = bf16[8,9216,384]{2,1,0:T(8,128)(2,1)} reshape(bf16[128,221184]{1,0:T(8,128)(2,1)} %convolution_convert_fusion) | data formatting | bytes 113246208 | tf_op jit(solution)/shard_map/reshape | solution.py:22
  158.6 483.0 %all-to-all-done = bf16[4,16,576,384]{3,2,1,0:T(8,128)(2,1)} async-done(((bf16[4,16,576,384]{3,2,1,0:T(8,128)(2,1)}), bf16[4,16,576,384]{3,2,1,0:T(8,128)(2,1)}, u32[]{:S(2)}, u32[]{:S(2)}) %all-to-all-start) | async-done | bytes 28311584 | tf_op jit(solution)/shard_map/all_to_all | solution.py:12
  641.6 0.0 copy-start.1
  641.6 98.8 %fusion.2 = f32[4,8,384,384]{3,2,0,1:T(8,128)} fusion(bf16[9216,4,384,1]{2,0,1,3:T(8,128)(2,1)} %bitcast.4, bf16[8,9216,384]{2,1,0:T(8,128)(2,1)} %reshape.19), kind=kOutput, calls=%fused_computation.3 | convolution fusion | flops 86973087744 | bytes 103809024 | tf_op jit(solution)/shard_map/ika,kcb->ciab/dot_general | solution.py:24
  740.4 12.6 %copy.6 = f32[4,8,384,384]{3,2,1,0:T(8,128)} copy(f32[4,8,384,384]{3,2,0,1:T(8,128)} %fusion.2) | data formatting | bytes 37748736 | tf_op jit(solution)/shard_map/ika,kcb->ciab/transpose | solution.py:24
  753.0 0.0 reduce-scatter.2.cloned.1.call-update
  753.0 125.8 %reduce-scatter.2.cloned.1.call-done = f32[4,384,384]{2,1,0:T(8,128)} async-done(((f32[32,384,384]{2,1,0:T(8,128)}), f32[4,384,384]{2,1,0:T(8,128)}) %reduce-scatter.2.cloned.1.call-update) | async-done | bytes 2359312 | tf_op jit(solution)/shard_map/reduce_scatter | solution.py:26
  878.8 0.0 copy-done.1
Async XLA Ops:
  6.5 63.7 %copy-start = (bf16[8,16,64]{2,1,0:T(8,128)(2,1)S(1)}, bf16[8,16,64]{2,1,0:T(8,128)(2,1)}, u32[]{:S(2)}) copy-start(bf16[8,16,64]{2,1,0:T(8,128)(2,1)} %param.5) | copy-start | bytes 49156
  21.0 620.6 %all-to-all-start = ((bf16[4,16,576,384]{3,2,1,0:T(8,128)(2,1)}), bf16[4,16,576,384]{3,2,1,0:T(8,128)(2,1)}, u32[]{:S(2)}, u32[]{:S(2)}) async-start(bf16[4,16,576,384]{3,2,1,0:T(8,128)(2,1)} %stack.2), calls=%async_computation | async-start | bytes 56623104 | tf_op jit(solution)/shard_map/all_to_all | solution.py:12
  29.9 848.9 %reduce-scatter.2.cloned.1.call-start = ((), (), s32[]{:S(2)}) async-start(), calls=%async_computation.2 | async-start | bytes 21233664 | tf_op jit(solution)/shard_map/reduce_scatter | solution.py:26
  641.6 237.2 %copy-start.1 = (bf16[8,16,64]{2,1,0:T(8,128)(2,1)S(1)}, bf16[8,16,64]{2,1,0:T(8,128)(2,1)}, u32[]{:S(2)}) copy-start(bf16[8,16,64]{2,1,0:T(8,128)(2,1)} %param.5) | copy-start | bytes 49156
Sparse Core Ops, SparseCore 0:
  753.2 125.5 reduce-scatter.1
